TPU v7x, 32 devices: a whole 2x2x4 slice. The times are simulated.
32 devices in a mesh: row: 4 (over y, core), col: 8 (over z, x).
Axes of the slice: x: 2, y: 2, z: 4, core: 2. Of those that a mesh axis runs over, the one named last changes fastest.
Arguments:
- amplitudes: float32 [256, 2, 16384], P('row', None, 'col'), may hold values from -6 to 6
- integrals: bfloat16 [2, 16384, 16384], P(None, 'col', 'row'), may hold values from -0.046875 to 0.046875
- screen: int32 [2, 128, 128], P(None, 'col', 'row'), may hold values 0 or 1
- mirror: int32 [16384], replicated, may hold values from 0 to 16383, as said below
- denominators: float32 [256, 2, 16384], P('col', None, 'row'), may hold values from 0.5 to 4
Outputs:
- update: float32 [256, 2, 16384], P('col', None, 'row')
Inputs may be any that keep to these rules, and one draw needn't show every extreme that they name: mirror is a permutation; mirror[p] lies in the tile of 128 positions numbered (p // 128 + 16384 // 256) modulo 16384 // 128.
All inputs are finite; a program needn't handle non-finite values. No bound on the sum of `screen` on one device may be relied on, other than what follows from the above.
Results may differ from a plain program's by a relative error of at most 0.0029.
Values may be sent and summed in bfloat16 or wider, within the bound.
A program may use at most 192 MiB of HBM per device.

v0:
```python
import jax
import jax.numpy as jnp
from jax import lax
from jax.sharding import PartitionSpec as P

TILE = 128


def partner_2(array, axis, stride):
    return lax.ppermute(array, axis, [(i, i ^ 1 << stride) for i in range(lax.axis_size(axis))])


def masked_integrals(integrals, screen):
    signs, cd_width, ab_width = integrals.shape
    blocks = integrals.reshape(signs, cd_width // TILE, TILE, ab_width // TILE, TILE)
    keep = screen.astype(integrals.dtype)[:, :, None, :, None]
    return (blocks * keep).reshape(signs, cd_width, ab_width)


def ordered_terms(signed, masked):
    plus_part = jnp.dot(signed[:, 0, :], masked[0], preferred_element_type=jnp.float32)
    minus_part = jnp.dot(signed[:, 1, :], masked[1], preferred_element_type=jnp.float32)
    return jnp.stack([0.5 * (plus_part + minus_part), 0.5 * (plus_part - minus_part)], axis=1)


def signed_pairs(direct, partner, local_index):
    flipped = jnp.take(partner, local_index, axis=1)
    return jnp.stack([direct + flipped, direct - flipped], axis=1).astype(jnp.bfloat16)


def body(amplitudes, integrals, screen, mirror, denominators):
    col_count = lax.axis_size("col")
    row_count = lax.axis_size("row")
    col_bit = col_count.bit_length() - 2
    row_bit = row_count.bit_length() - 2
    cd_width = amplitudes.shape[2]
    ab_width = denominators.shape[2]
    col_place = lax.axis_index("col")
    row_place = lax.axis_index("row")
    cd_start = col_place * cd_width
    cd_partner = (col_place + col_count // 2) % col_count * cd_width
    cd_index = lax.dynamic_slice_in_dim(mirror, cd_start, cd_width) - cd_partner
    masked = masked_integrals(integrals, screen)
    terms = None
    partner = partner_2(amplitudes[:, 1, :], "col", col_bit)
    own_signed = signed_pairs(amplitudes[:, 0, :], partner, cd_index)
    terms = ordered_terms(lax.all_gather(own_signed, "row", axis=0, tiled=True), masked)
    summed = lax.psum_scatter(terms, "col", scatter_dimension=0, tiled=True)
    direct_part = summed[:, 0, :]
    mirrored = partner_2(summed[:, 1, :], "row", row_bit)
    ab_start = row_place * ab_width
    ab_partner = (row_place + row_count // 2) % row_count * ab_width
    placed = lax.dynamic_slice_in_dim(mirror, ab_partner, ab_width) - ab_start
    mirror_part = jnp.zeros_like(mirrored).at[:, placed].set(mirrored)
    residual = jnp.stack([direct_part, mirror_part], axis=1)
    return residual / denominators


def solution(mesh):
    in_specs = (
        P("row", None, "col"),
        P(None, "col", "row"),
        P(None, "col", "row"),
        P(),
        P("col", None, "row"),
    )
    out_specs = P("col", None, "row")
    return jax.shard_map(body, mesh=mesh, in_specs=in_specs, out_specs=out_specs, check_vma=False)
```

profile of v0, /device:TPU:0, one launch (start us, length us, event | category | flops | bytes accessed | tf_op | source)
XLA Modules:
  0.0 315.6 jit_solution(2353124058427291966)
XLA Ops:
  6.5 0.0 all-gather.2.cloned.1.call-start
  6.5 2.7 fusion.12
  9.2 0.2 copy.55
  9.4 4.1 %collective-permute-start = (f32[64,2048]{1,0:T(8,128)S(1)}, f32[64,2048]{1,0:T(8,128)S(1)}, u32[]{:S(2)}, u32[]{:S(2)}) collective-permute-start(f32[64,2048]{1,0:T(8,128)S(1)} %bitcast.49), channel_id=1, source_target_pairs={{0,4},{1,5},{2,6},{3,7},{4,0},{5,1},{6,2},{7,3},{8,12},{9,13},{10,... | collective-permute-start | bytes 1572872 | tf_op jit(solution)/shard_map/ppermute | solution.py:10
  13.5 0.0 copy-start
  13.5 0.0 copy-start.1
  13.5 23.1 %copy.34 = bf16[512,8,32,128]{3,2,1,0:T(8,128)(2,1)} copy(bf16[512,8,32,128]{3,1,2,0:T(8,128)(2,1)} %bitcast.44) | data formatting | bytes 67108864
  36.6 0.0 copy-done
  36.6 0.5 copy.30
  37.1 0.0 copy-done.1
  37.2 0.0 collective-permute-done
  37.2 0.3 copy.22
  37.6 5.5 %gather_fusion = f32[2048,64]{1,0:T(8,128)S(1)} fusion(f32[64,2048]{0,1:T(8,128)S(1)} %copy.22, s32[2048]{0:T(1024)S(1)} %fusion.8), kind=kCustom, calls=%fused_computation | custom fusion | bytes 1056768 | tf_op jit(solution)/shard_map/jit(_take)/gather | solution.py:27
  43.0 0.5 add_convert_fusion
  43.5 0.2 pad_maximum_fusion.1
  43.7 1.3 copy.23
  45.1 0.0 all-gather.2.cloned.1.call-update
  45.1 0.2 reduce-scatter.2.cloned.1.call-start
  45.3 23.9 %broadcast_multiply_fusion = bf16[2,16,128,32,128]{4,3,2,1,0:T(8,128)(2,1)} fusion(bf16[2,16,128,32,128]{4,3,2,1,0:T(8,128)(2,1)} %bitcast.43, bf16[2,16,32]{2,1,0:T(8,128)(2,1)S(1)} %convert_element_type.4), kind=kLoop, calls=%fused_computation.8 | loop fusion | flops 16777216 | bytes 67110912 | tf_op jit(solution)/shard_map/mul | solution.py:17
  69.2 24.7 %fusion.9 = (bf16[1,16,128,32,128]{4,3,2,1,0:T(8,128)(2,1)}, bf16[1,16,128,32,128]{4,3,2,1,0:T(8,128)(2,1)}) fusion(bf16[2,16,128,32,128]{4,3,2,1,0:T(8,128)(2,1)} %broadcast_multiply_fusion), kind=kLoop, calls=%fused_computation.27 | loop fusion | bytes 67108864 | tf_op jit(solution)/shard_map/slice | solution.py:22
  93.9 0.0 all-gather.2.cloned.1.call-done
  93.9 5.6 %fusion.10 = (bf16[256,1,2048]{2,1,0:T(2,128)(2,1)S(1)}, bf16[256,1,2048]{2,1,0:T(2,128)(2,1)S(1)}) fusion(bf16[256,2,2048]{2,1,0:T(2,128)(2,1)} %all-gather.2.cloned.1.call-done), kind=kLoop, calls=%fused_computation.28 | loop fusion | bytes 4194304 | tf_op jit(solution)/shard_map/slice | solution.py:22
  99.5 12.1 %fusion = f32[256,4096]{1,0:T(8,128)S(1)} fusion(bf16[256,8,32,128]{3,2,1,0:T(8,128)(2,1)} %bitcast.46, bf16[256,1,2048]{2,1,0:T(2,128)(2,1)S(1)} %get-tuple-element.11), kind=kOutput, calls=%fused_computation.2 | convolution fusion | flops 4294967296 | bytes 22020096 | tf_op jit(solution)/shard_map/dot_general | solution.py:22
  111.6 12.1 %multiply_bitcast_fusion.1 = (f32[256,1,4096]{2,0,1:T(8,128)S(1)}, f32[256,1,4096]{2,0,1:T(8,128)S(1)}) fusion(f32[256,4096]{1,0:T(8,128)S(1)} %fusion, bf16[256,8,32,128]{3,2,1,0:T(8,128)(2,1)} %bitcast.45, bf16[256,1,2048]{2,1,0:T(2,128)(2,1)S(1)} %get-tuple-element.12), kind=kOutput, calls=%fused_computation.11 | convolution fusion | flops 4299161600 | bytes 30408704 | tf_op jit(solution)/shard_map/dot_general | solution.py:21
  123.8 4.2 %pad_maximum_fusion = f32[256,2,4096]{2,0,1:T(8,128)} fusion(f32[256,1,4096]{2,0,1:T(8,128)S(1)} %get-tuple-element.8, f32[256,1,4096]{2,0,1:T(8,128)S(1)} %get-tuple-element.7), kind=kLoop, calls=%fused_computation.9 | loop fusion | flops 2097152 | bytes 16777216 | tf_op jit(solution)/shard_map/stack | solution.py:23
  128.0 0.0 reduce-scatter.2.cloned.1.call-update
  128.0 148.2 %reduce-scatter.2.cloned.1.call-done = f32[32,2,4096]{2,0,1:T(8,128)} async-done(((f32[256,2,4096]{2,0,1:T(8,128)}), f32[32,2,4096]{2,0,1:T(8,128)}) %reduce-scatter.2.cloned.1.call-update) | async-done | bytes 1048592 | tf_op jit(solution)/shard_map/reduce_scatter | solution.py:48
  276.2 1.3 fusion.11
  277.5 1.5 collective-permute-start.1
  279.0 11.9 %collective-permute-done.1 = f32[32,4096]{1,0:T(8,128)S(1)} collective-permute-done((f32[32,4096]{1,0:T(8,128)S(1)}, f32[32,4096]{1,0:T(8,128)S(1)}, u32[]{:S(2)}, u32[]{:S(2)}) %collective-permute-start.1) | collective-permute-done | bytes 524320 | tf_op jit(solution)/shard_map/ppermute | solution.py:10
  290.9 1.9 copy.26
  292.9 11.6 %scatter_custom_fusion = f32[32,4096]{0,1:T(8,128)S(1)} fusion(s32[4096]{0:T(1024)S(1)} %compare_select_fusion, f32[4096,32]{1,0:T(8,128)} %copy.26, f32[]{:T(128)} %constant.55.clone.1), kind=kCustom, calls=%fused_computation.17 | custom fusion | bytes 524800 | tf_op jit(solution)/shard_map/scatter | solution.py:54
  304.5 0.6 copy.27
  305.1 1.9 maximum_divide_fusion
  307.0 1.8 copy.29
  (4 shorter events, 0.0 us)
Async XLA Ops:
  6.5 87.4 %all-gather.2.cloned.1.call-start = ((), (), s32[]{:S(2)}) async-start(), calls=%async_computation.1 | async-start | bytes 2621440 | tf_op jit(solution)/shard_map/all_gather | solution.py:47
  9.4 27.8 %collective-permute-start = (f32[64,2048]{1,0:T(8,128)S(1)}, f32[64,2048]{1,0:T(8,128)S(1)}, u32[]{:S(2)}, u32[]{:S(2)}) collective-permute-start(f32[64,2048]{1,0:T(8,128)S(1)} %bitcast.49), channel_id=1, source_target_pairs={{0,4},{1,5},{2,6},{3,7},{4,0},{5,1},{6,2},{7,3},{8,12},{9,13},{10,... | collective-permute-start | bytes 1572872 | tf_op jit(solution)/shard_map/ppermute | solution.py:10
  13.5 23.1 %copy-start = (s32[2,16,32]{2,1,0:T(8,128)S(1)}, s32[2,16,32]{2,1,0:T(8,128)}, u32[]{:S(2)}) copy-start(s32[2,16,32]{2,1,0:T(8,128)} %param.7) | copy-start | bytes 12292
  13.5 23.6 %copy-start.1 = (s32[16384]{0:T(1024)S(1)}, s32[16384]{0:T(1024)}, u32[]{:S(2)}) copy-start(s32[16384]{0:T(1024)} %param.8) | copy-start | bytes 196612
  45.1 231.1 %reduce-scatter.2.cloned.1.call-start = ((), (), s32[]{:S(2)}) async-start(), calls=%async_computation.2 | async-start | bytes 9437184 | tf_op jit(solution)/shard_map/reduce_scatter | solution.py:48
  277.5 13.4 %collective-permute-start.1 = (f32[32,4096]{1,0:T(8,128)S(1)}, f32[32,4096]{1,0:T(8,128)S(1)}, u32[]{:S(2)}, u32[]{:S(2)}) collective-permute-start(f32[32,4096]{1,0:T(8,128)S(1)} %get-tuple-element.14), channel_id=1, source_target_pairs={{0,16},{8,24},{16,0},{24,8},{1,17},{9,25},{17,1},{25,9},{2,18},{10... | collective-permute-start | bytes 1572872 | tf_op jit(solution)/shard_map/ppermute | solution.py:10
Sparse Core Ops, SparseCore 0:
  45.2 23.2 all-gather.1
  128.1 148.0 reduce-scatter.1
where the time goes:
time: 316 us
  waiting for transfers between devices  160 us (51%)
  local copies, waits for them, and re-layouts  81.1 us (26%)
  other arithmetic  30.7 us (10%)
  matrix products  24.2 us (8%)
  between operations  13.6 us (4%)
  starting transfers between devices  5.89 us (2%)
    reduce_scatter x1, waiting for transfers between devices, body(): summed = lax.psum_scatter(terms, 'col', scatter_dimension=0, tiled=True)  148 us
    slice x1, local copies, waits for them, and re-layouts, ordered_terms(): masked[1]  24.7 us
    mul x1, other arithmetic, masked_integrals(): return (blocks * keep).reshape(signs, cd_width, ab_width)  23.9 us
    unnamed x7, local copies, waits for them, and re-layouts  23.7 us
    scatter x2, local copies, waits for them, and re-layouts, body(): mirror_part = jnp.zeros_like(mirrored).at[:, placed].set(mirrored)  12.2 us
    dot_general x1, matrix products, ordered_terms(): jnp.dot(signed[:, 0, :], masked[0], preferred_element_type=jnp.float32)  12.1 us
    dot_general x1, matrix products, ordered_terms(): jnp.dot(signed[:, 1, :], masked[1], preferred_element_type=jnp.float32)  12.1 us
    ppermute x2, waiting for transfers between devices, partner_2(): lax.ppermute(array, axis, [(i, i ^ 1 << stride) for i in range(lax.axis_s...  11.9 us
  transfers between devices with their start and end apart: 4, of which 2 were waited for; matrix products, arithmetic and copies ran while one was open for 23% of the time, Pallas kernels for 0%

commit v1 on v0

v1 whole, which is shorter than its diff:
```python
import functools

import jax
import jax.numpy as jnp
from jax import lax
from jax.experimental import pallas as pl
from jax.experimental.pallas import tpu as pltpu
from jax.sharding import PartitionSpec as P

TILE = 128
F32, BF16 = jnp.float32, jnp.bfloat16


def flip(x, bits):
    result = x
    place = 0
    while bits >> place:
        if bits >> place & 1:
            result = result + (1 - 2 * (x // (1 << place) % 2)) * (1 << place)
        place += 1
    return result


def position(owner, me, bits):
    total = 0
    for i in range(bits):
        differs = (owner // (1 << i) + me // (1 << i)) % 2
        total = total + differs * (1 << (bits - 1 - i))
    return total


def kernel(sizes, direct, mirrored, cd_lane, ab_lane, mask, integrals, out0, out1,
           held, arrived, signed, acc, *rest):
    rows, cols, groups, chunk = sizes
    row_bits, col_bits = rows.bit_length() - 1, cols.bit_length() - 1
    sends, recvs = rest[:col_bits], rest[col_bits:2 * col_bits]
    msend, mrecv, k_sem, f_sem, g_sem, r_sem, m_sem = rest[2 * col_bits:]
    occ, cd_width = direct.shape
    ab_width = out0.shape[1]
    own = out0.shape[0]
    part = own // groups
    per_row = occ // own
    chunks = ab_width // chunk
    pieces = groups * chunks
    row_me, col_me = lax.axis_index("row"), lax.axis_index("col")

    barrier = pltpu.get_barrier_semaphore()
    for b in range(col_bits):
        pl.semaphore_signal(barrier, inc=1, device_id={"col": flip(col_me, 1 << b)}, device_id_type=pl.DeviceIdType.MESH)
    for b in range(row_bits):
        pl.semaphore_signal(barrier, inc=1, device_id={"row": flip(row_me, 1 << b)}, device_id_type=pl.DeviceIdType.MESH)
    pl.semaphore_wait(barrier, col_bits + row_bits)

    def remote(src, dst, sem, target):
        return pltpu.make_async_remote_copy(
            src_ref=src, dst_ref=dst, send_sem=sem[0], recv_sem=sem[1],
            device_id=target, device_id_type=pl.DeviceIdType.MESH)

    def f_copy(g, k):
        at = pl.ds(k * own + g * part, part)
        i = g * per_row + k
        return remote(mirrored.at[at, :], arrived.at[at, :], (f_sem.at[0, i], f_sem.at[1, i]),
                      {"col": flip(col_me, cols // 2)})

    def k_copy(j):
        c, s = j // 2, j % 2
        return pltpu.make_async_copy(
            integrals.at[s, :, pl.ds(pl.multiple_of(c * chunk, chunk), chunk)], held.at[j], k_sem.at[j])

    def gather_copies(g, stage, k):
        bit = row_bits - 1 - stage
        copies = []
        for t in range(1 << stage):
            shard = flip(row_me, t << (bit + 1))
            pos = position(shard * per_row + k, col_me, col_bits)
            i = (g * rows + (1 << stage) - 1 + t) * per_row + k
            block = signed.at[g, :, pos]
            copies.append(remote(block, block, (g_sem.at[0, i], g_sem.at[1, i]), {"row": flip(row_me, 1 << bit)}))
        return copies

    def keep_tiles(j):
        c, s = j // 2, j % 2
        k_copy(j).wait()

        def one(t, carry):
            factor = mask[s, pl.ds(t, 1), pl.ds(pl.multiple_of(c * chunk, chunk), chunk)]
            factor = jnp.broadcast_to(factor, (16, chunk)).astype(BF16)
            at = pl.ds(pl.multiple_of(t * TILE, TILE), TILE)
            block = held[j, at, :].reshape(TILE // 16, 16, chunk)
            held[j, at, :] = (block * factor[None]).reshape(TILE, chunk)
            return carry

        lax.fori_loop(0, cd_width // TILE, one, 0)

    def make_signed(g, k):
        f_copy(g, k).wait()
        pos = position(row_me * per_row + k, col_me, col_bits)
        at = pl.ds(k * own + g * part, part)
        for t in range(cd_width // TILE):
            lanes = pl.ds(t * TILE, TILE)
            index = jnp.broadcast_to(cd_lane[pl.ds(t, 1), :], (part, TILE))
            flipped = jnp.take_along_axis(arrived[at, lanes], index, axis=1)
            mine = direct[at, lanes]
            signed[g, 0, pos, :, lanes] = (mine + flipped).astype(BF16)
            signed[g, 1, pos, :, lanes] = (mine - flipped).astype(BF16)

    for g in range(groups):
        for k in range(per_row):
            f_copy(g, k).start()

    def start_k(j, carry):
        k_copy(j).start()
        return carry

    lax.fori_loop(0, 2 * chunks, start_k, 0)

    for k in range(per_row):
        lo, hi = 2 * chunks * k // per_row, 2 * chunks * (k + 1) // per_row

        def keep_step(j, carry):
            keep_tiles(j)
            return carry

        lax.fori_loop(lo, hi, keep_step, 0)
        make_signed(0, k)
        for copy in gather_copies(0, 0, k):
            copy.start()

    def gather_event(g, stage):
        for k in range(per_row):
            if stage == 0:
                make_signed(g, k)
            else:
                for copy in gather_copies(g, stage - 1, k):
                    copy.wait()
            if stage < row_bits:
                for copy in gather_copies(g, stage, k):
                    copy.start()

    for stage in range(1, row_bits + 1):
        gather_event(0, stage)

    def stage_copy(b, q):
        return remote(sends[b].at[q], recvs[b].at[q], (r_sem.at[0, b, q], r_sem.at[1, b, q]),
                      {"col": flip(col_me, 1 << b)})

    def mirror_copy(q):
        return remote(msend.at[q], mrecv.at[q], (m_sem.at[0, q], m_sem.at[1, q]),
                      {"row": flip(row_me, rows // 2)})

    def multiply(q):
        g, c = q // chunks, q % chunks
        for s in range(2):
            lhs = signed[g, s].reshape(cols * part, cd_width)
            total = jnp.dot(lhs, held[2 * c + s], preferred_element_type=F32)
            half = cols * part // 2
            acc[q, s] = total[:half]
            sends[0][q, s] = total[half:].astype(BF16)
        stage_copy(0, q).start()

    def reduce(b, q):
        stage_copy(b - 1, q).wait()
        half = (cols >> b) * part // 2
        for s in range(2):
            sends[b][q, s] = (acc[q, s, half:2 * half] + recvs[b - 1][q, s, half:2 * half].astype(F32)).astype(BF16)
            acc[q, s, :half] = acc[q, s, :half] + recvs[b - 1][q, s, :half].astype(F32)
        stage_copy(b, q).start()

    def combine(q):
        g, c = q // chunks, q % chunks
        stage_copy(col_bits - 1, q).wait()
        plus = acc[q, 0, :part] + recvs[-1][q, 0].astype(F32)
        minus = acc[q, 1, :part] + recvs[-1][q, 1].astype(F32)
        out0[pl.ds(pl.multiple_of(g * part, part), part), pl.ds(pl.multiple_of(c * chunk, chunk), chunk)] = 0.5 * (plus + minus)
        msend[q] = (0.5 * (plus - minus)).astype(BF16)
        mirror_copy(q).start()

    def place(q):
        g, c = q // chunks, q % chunks
        mirror_copy(q).wait()
        for t in range(chunk // TILE):
            target = jnp.broadcast_to(ab_lane[pl.ds(c * (chunk // TILE) + t, 1), :], (TILE, TILE))
            hit = lax.broadcasted_iota(jnp.int32, (TILE, TILE), 0) == target
            chosen = jnp.where(hit, 1.0, 0.0).astype(BF16)
            moved = lax.dot_general(mrecv[q, :, pl.ds(t * TILE, TILE)], chosen, (((1,), (1,)), ((), ())), preferred_element_type=F32)
            out1[pl.ds(pl.multiple_of(g * part, part), part),
                 pl.ds(pl.multiple_of(c * chunk + t * TILE, TILE), TILE)] = moved

    def step(i, carry):
        for g in range(1, groups):
            for stage in range(row_bits + 1):
                when = g * chunks - (0 if stage == row_bits else row_bits + 1 - stage)

                @pl.when(i == when)
                def _():
                    gather_event(g, stage)

        @pl.when(i < pieces)
        def _():
            multiply(i)

        lag = 0
        for b in range(1, col_bits):
            lag += 2 if b == 1 else 1

            @pl.when((i >= lag) & (i < pieces + lag))
            def _():
                reduce(b, i - lag)

        lag += 1

        @pl.when((i >= lag) & (i < pieces + lag))
        def _():
            combine(i - lag)

        lag += 1

        @pl.when((i >= lag) & (i < pieces + lag))
        def _():
            place(i - lag)

        return carry

    lax.fori_loop(0, pieces + col_bits + 2, step, 0)


def body(amplitudes, integrals, screen, mirror, denominators):
    cols, rows = lax.axis_size("col"), lax.axis_size("row")
    col_bits = cols.bit_length() - 1
    occ, _, cd_width = amplitudes.shape
    own, _, ab_width = denominators.shape
    per_row = occ // own
    groups = 2 if own % 32 == 0 else 1
    part = own // groups
    chunk = min(512, ab_width)
    chunks = ab_width // chunk
    pieces = groups * chunks
    ab_partner = (lax.axis_index("row") + rows // 2) % rows * ab_width
    lanes = mirror % TILE
    cd_lane = lax.dynamic_slice_in_dim(lanes, lax.axis_index("col") * cd_width, cd_width).reshape(-1, TILE)
    ab_lane = lax.dynamic_slice_in_dim(lanes, ab_partner, ab_width).reshape(-1, TILE)
    mask = jnp.repeat(screen.astype(F32), TILE, axis=2)
    vmem = pl.BlockSpec(memory_space=pltpu.VMEM)
    shape = lambda b: (pieces, 2, (cols >> b + 1) * part, chunk)
    out0, out1 = pl.pallas_call(
        functools.partial(kernel, (rows, cols, groups, chunk)),
        out_shape=[jax.ShapeDtypeStruct((own, ab_width), F32)] * 2,
        in_specs=[vmem] * 5 + [pl.BlockSpec(memory_space=pl.ANY)],
        out_specs=[vmem] * 2,
        scratch_shapes=[
            pltpu.VMEM((2 * chunks, cd_width, chunk), BF16),
            pltpu.VMEM((occ, cd_width), F32),
            pltpu.VMEM((groups, 2, cols, part, cd_width), BF16),
            pltpu.VMEM(shape(0), F32),
        ] + [pltpu.VMEM(shape(b), BF16) for b in range(col_bits)] * 2 + [
            pltpu.VMEM((pieces, part, chunk), BF16),
            pltpu.VMEM((pieces, part, chunk), BF16),
            pltpu.SemaphoreType.DMA((2 * chunks,)),
            pltpu.SemaphoreType.DMA((2, groups * per_row)),
            pltpu.SemaphoreType.DMA((2, groups * rows * per_row)),
            pltpu.SemaphoreType.DMA((2, col_bits, pieces)),
            pltpu.SemaphoreType.DMA((2, pieces)),
        ],
        compiler_params=pltpu.CompilerParams(
            collective_id=0, has_side_effects=True, vmem_limit_bytes=60 * 1024 * 1024),
    )(amplitudes[:, 0, :], amplitudes[:, 1, :], cd_lane, ab_lane, mask, integrals)
    return jnp.stack([out0, out1], axis=1) / denominators


def solution(mesh):
    in_specs = (
        P("row", None, "col"),
        P(None, "col", "row"),
        P(None, "col", "row"),
        P(),
        P("col", None, "row"),
    )
    out_specs = P("col", None, "row")
    return jax.shard_map(body, mesh=mesh, in_specs=in_specs, out_specs=out_specs, check_vma=False)
```

time: 316 us -> 106 us (0.34)
  waiting for transfers between devices: 160 us -> 0 us
  Pallas kernels: 0 us -> 94 us
  local copies, waits for them, and re-layouts: 81.1 us -> 7.97 us
  other arithmetic: 30.7 us -> 3.51 us
  matrix products: 24.2 us -> 0 us
  between operations: 13.6 us -> 0.03 us
  starting transfers between devices: 5.89 us -> 0 us
    reduce_scatter x1 -> x0, waiting for transfers between devices: 148 us -> none  [body(): summed = lax.psum_scatter(terms, 'col', scatter_dimension=0, tiled=True)]
    pallas_call x0 -> x1, Pallas kernels: none -> 94 us  [body(): pl.pallas_call(functools.partial(kernel, (rows, cols, groups, chunk)), ou...]
    slice x4 -> x1, local copies, waits for them, and re-layouts: 34.3 us -> 2.61 us  [body(): amplitudes[:, 1, :]]
    dot_general x2 -> x0, matrix products: 24.2 us -> none  [the longest x1 12.1 us: ordered_terms(): jnp.dot(signed[:, 0, :], masked[0], preferred_element_type=jnp.float32)]
    mul x1 -> x0, other arithmetic: 23.9 us -> none  [masked_integrals(): return (blocks * keep).reshape(signs, cd_width, ab_width)]
    unnamed x7 -> x2, local copies, waits for them, and re-layouts: 23.7 us -> 0.01 us
    scatter x2 -> x0, local copies, waits for them, and re-layouts: 12.2 us -> none  [body(): mirror_part = jnp.zeros_like(mirrored).at[:, placed].set(mirrored)]
    ppermute x2 -> x0, waiting for transfers between devices: 11.9 us -> none  [partner_2(): lax.ppermute(array, axis, [(i, i ^ 1 << stride) for i in range(lax.axis_s...]
  transfers between devices with their start and end apart: 4 -> 0, of which waited for: 2 -> 0; matrix products, arithmetic and copies ran while one was open for 23% -> 0% of each run, Pallas kernels for 0% -> 0%
where the time goes in v1:
time: 106 us; the launch traced here: 105 us
  Pallas kernels  94 us (89%)
  local copies, waits for them, and re-layouts  7.97 us (8%)
  other arithmetic  3.51 us (3%)
    pallas_call x1, Pallas kernels, body(): pl.pallas_call(functools.partial(kernel, (rows, cols, groups, chunk)), ou...  94 us
    slice x1, local copies, waits for them, and re-layouts, body(): amplitudes[:, 1, :]  2.61 us

profile of v1, /device:TPU:0, one launch (start us, length us, event | category | flops | bytes accessed | tf_op | source)
XLA Modules:
  0.0 105.5 jit_solution(8978859721305154107)
XLA Ops:
  0.0 0.0 copy-start
  0.0 0.8 convert_element_type.3
  0.8 0.9 add_select_fusion
  1.7 0.6 dynamic-slice_bitcast_fusion.1.cd_lane
  2.3 0.6 dynamic-slice_bitcast_fusion.ab_lane
  2.9 0.2 broadcast_in_dim.3
  3.1 0.9 reshape.11.mask
  4.0 2.6 %fusion.1 = (f32[64,1,2048]{2,1,0:T(1,128)S(1)}, f32[64,1,2048]{2,1,0:T(1,128)S(1)}) fusion(f32[64,2,2048]{2,1,0:T(2,128)} %param.5), kind=kLoop, calls=%fused_computation.9 | loop fusion | bytes 2097152 | tf_op jit(solution)/shard_map/slice | solution.py:266
  6.6 1.3 %copy_bitcast_fusion = (f32[64,2048]{1,0:T(8,128)}, f32[64,2048]{1,0:T(8,128)}) fusion(f32[64,1,2048]{2,1,0:T(1,128)S(1)} %get-tuple-element.9, f32[64,1,2048]{2,1,0:T(1,128)S(1)} %get-tuple-element.10), kind=kLoop, calls=%fused_computation.1 | loop fusion | bytes 2097152 | tf_op jit(solution)/shard_map/squeeze | solution.py:266
  7.9 94.0 %shard_map.55 = (f32[32,4096]{1,0:T(8,128)}, f32[32,4096]{1,0:T(8,128)}) custom-call(f32[64,2048]{1,0:T(8,128)} %get-tuple-element.12.direct, f32[64,2048]{1,0:T(8,128)} %get-tuple-element.11.mirrored, s32[16,128]{1,0:T(8,128)} %dynamic-slice_bitcast_fusion.1.cd_lane, s32[32,128]{1,0:T(8,128)} %dynamic-slice_bitcast_fusion.ab_lane, ...), custom_call_target="tpu_custom_call" | custom-call | tf_op jit(solution)/shard_map/pallas_call | solution.py:245
  101.9 0.0 copy-done
  101.9 1.8 %maximum_divide_fusion = f32[32,2,4096]{2,0,1:T(8,128)S(1)} fusion(f32[32,1,4096]{2,0,1:T(8,128)} %bitcast.13, f32[32,1,4096]{2,0,1:T(8,128)} %bitcast.12, f32[32,2,4096]{2,1,0:T(2,128)S(1)} %copy-done), kind=kLoop, calls=%fused_computation | loop fusion | flops 524288 | bytes 3145728 | tf_op jit(solution)/shard_map/div | solution.py:267
  103.7 1.8 %copy.9 = f32[32,2,4096]{2,1,0:T(2,128)} copy(f32[32,2,4096]{2,0,1:T(8,128)S(1)} %maximum_divide_fusion) | data formatting | bytes 2097152 | tf_op jit(solution)/shard_map/div | solution.py:267
Async XLA Ops:
  0.0 101.9 %copy-start = (f32[32,2,4096]{2,1,0:T(2,128)S(1)}, f32[32,2,4096]{2,1,0:T(2,128)}, u32[]{:S(2)}) copy-start(f32[32,2,4096]{2,1,0:T(2,128)} %param.9) | copy-start | bytes 3145732

commit v2 on v1

--- a/solution.py
+++ b/solution.py
@@ -29,7 +29,7 @@
     return total
 
 
-def kernel(sizes, direct, mirrored, cd_lane, ab_lane, mask, integrals, out0, out1,
+def kernel(sizes, direct, mirrored, mirror, mask, integrals, out0, out1,
            held, arrived, signed, acc, *rest):
     rows, cols, groups, chunk = sizes
     row_bits, col_bits = rows.bit_length() - 1, cols.bit_length() - 1
@@ -84,7 +84,7 @@
 
         def one(t, carry):
             factor = mask[s, pl.ds(t, 1), pl.ds(pl.multiple_of(c * chunk, chunk), chunk)]
-            factor = jnp.broadcast_to(factor, (16, chunk)).astype(BF16)
+            factor = jnp.broadcast_to(factor, (16, chunk)).astype(F32).astype(BF16)
             at = pl.ds(pl.multiple_of(t * TILE, TILE), TILE)
             block = held[j, at, :].reshape(TILE // 16, 16, chunk)
             held[j, at, :] = (block * factor[None]).reshape(TILE, chunk)
@@ -98,7 +98,7 @@
         at = pl.ds(k * own + g * part, part)
         for t in range(cd_width // TILE):
             lanes = pl.ds(t * TILE, TILE)
-            index = jnp.broadcast_to(cd_lane[pl.ds(t, 1), :], (part, TILE))
+            index = jnp.broadcast_to(mirror[pl.ds(col_me * (cd_width // TILE) + t, 1), :] % TILE, (part, TILE))
             flipped = jnp.take_along_axis(arrived[at, lanes], index, axis=1)
             mine = direct[at, lanes]
             signed[g, 0, pos, :, lanes] = (mine + flipped).astype(BF16)
@@ -179,7 +179,8 @@
         g, c = q // chunks, q % chunks
         mirror_copy(q).wait()
         for t in range(chunk // TILE):
-            target = jnp.broadcast_to(ab_lane[pl.ds(c * (chunk // TILE) + t, 1), :], (TILE, TILE))
+            at = flip(row_me, rows // 2) * (ab_width // TILE) + c * (chunk // TILE) + t
+            target = jnp.broadcast_to(mirror[pl.ds(at, 1), :] % TILE, (TILE, TILE))
             hit = lax.broadcasted_iota(jnp.int32, (TILE, TILE), 0) == target
             chosen = jnp.where(hit, 1.0, 0.0).astype(BF16)
             moved = lax.dot_general(mrecv[q, :, pl.ds(t * TILE, TILE)], chosen, (((1,), (1,)), ((), ())), preferred_element_type=F32)
@@ -232,20 +233,15 @@
     per_row = occ // own
     groups = 2 if own % 32 == 0 else 1
     part = own // groups
-    chunk = min(512, ab_width)
+    chunk = min(1024, ab_width)
     chunks = ab_width // chunk
     pieces = groups * chunks
-    ab_partner = (lax.axis_index("row") + rows // 2) % rows * ab_width
-    lanes = mirror % TILE
-    cd_lane = lax.dynamic_slice_in_dim(lanes, lax.axis_index("col") * cd_width, cd_width).reshape(-1, TILE)
-    ab_lane = lax.dynamic_slice_in_dim(lanes, ab_partner, ab_width).reshape(-1, TILE)
-    mask = jnp.repeat(screen.astype(F32), TILE, axis=2)
     vmem = pl.BlockSpec(memory_space=pltpu.VMEM)
     shape = lambda b: (pieces, 2, (cols >> b + 1) * part, chunk)
     out0, out1 = pl.pallas_call(
         functools.partial(kernel, (rows, cols, groups, chunk)),
         out_shape=[jax.ShapeDtypeStruct((own, ab_width), F32)] * 2,
-        in_specs=[vmem] * 5 + [pl.BlockSpec(memory_space=pl.ANY)],
+        in_specs=[vmem] * 4 + [pl.BlockSpec(memory_space=pl.ANY)],
         out_specs=[vmem] * 2,
         scratch_shapes=[
             pltpu.VMEM((2 * chunks, cd_width, chunk), BF16),
@@ -263,7 +259,7 @@
         ],
         compiler_params=pltpu.CompilerParams(
             collective_id=0, has_side_effects=True, vmem_limit_bytes=60 * 1024 * 1024),
-    )(amplitudes[:, 0, :], amplitudes[:, 1, :], cd_lane, ab_lane, mask, integrals)
+    )(amplitudes[:, 0, :], amplitudes[:, 1, :], mirror.reshape(-1, TILE), jnp.repeat(screen, TILE, axis=2), integrals)
     return jnp.stack([out0, out1], axis=1) / denominators
 
 

time: 106 us -> 104 us (0.981)
  other arithmetic: 3.51 us -> 1.83 us
    reshape x3 -> x1, local copies, waits for them, and re-layouts: 2.08 us -> 0.89 us  [body(): jnp.repeat(screen, TILE, axis=2)]
where the time goes in v2:
time: 104 us
  Pallas kernels  94.2 us (91%)
  local copies, waits for them, and re-layouts  7.58 us (7%)
  other arithmetic  1.83 us (2%)
    pallas_call x1, Pallas kernels, body(): pl.pallas_call(functools.partial(kernel, (rows, cols, groups, chunk)), ou...  94.2 us
    slice x1, local copies, waits for them, and re-layouts, body(): amplitudes[:, 1, :]  2.61 us

profile of v2, /device:TPU:0, one launch (start us, length us, event | category | flops | bytes accessed | tf_op | source)
XLA Modules:
  0.0 103.7 jit_solution(8156894286714818710)
XLA Ops:
  0.0 0.0 copy-start
  0.0 1.0 broadcast_in_dim.3
  1.0 0.9 reshape.7.mask
  1.9 2.6 %fusion = (f32[64,1,2048]{2,1,0:T(1,128)S(1)}, f32[64,1,2048]{2,1,0:T(1,128)S(1)}) fusion(f32[64,2,2048]{2,1,0:T(2,128)} %param.5), kind=kLoop, calls=%fused_computation.3 | loop fusion | bytes 2097152 | tf_op jit(solution)/shard_map/slice | solution.py:262
  4.5 1.3 %copy_bitcast_fusion = (f32[64,2048]{1,0:T(8,128)}, f32[64,2048]{1,0:T(8,128)}) fusion(f32[64,1,2048]{2,1,0:T(1,128)S(1)} %get-tuple-element.9, f32[64,1,2048]{2,1,0:T(1,128)S(1)} %get-tuple-element.10), kind=kLoop, calls=%fused_computation.1 | loop fusion | bytes 2097152 | tf_op jit(solution)/shard_map/squeeze | solution.py:262
  5.8 94.2 %shard_map.55 = (f32[32,4096]{1,0:T(8,128)}, f32[32,4096]{1,0:T(8,128)}) custom-call(f32[64,2048]{1,0:T(8,128)} %get-tuple-element.12.direct, f32[64,2048]{1,0:T(8,128)} %get-tuple-element.11.mirrored, s32[128,128]{1,0:T(8,128)} %bitcast.11, s32[2,16,4096]{2,1,0:T(8,128)} %reshape.7.mask, bf16[2,2048,4096]{2,1,0:T(8,128)(2,1)} %integrals.1), custom_call_target="tpu_custom_call" | custom-call | tf_op jit(solution)/shard_map/pallas_call | solution.py:241
  100.0 0.0 copy-done
  100.0 1.8 %maximum_divide_fusion = f32[32,2,4096]{2,0,1:T(8,128)S(1)} fusion(f32[32,1,4096]{2,0,1:T(8,128)} %bitcast.10, f32[32,1,4096]{2,0,1:T(8,128)} %bitcast.9, f32[32,2,4096]{2,1,0:T(2,128)S(1)} %copy-done), kind=kLoop, calls=%fused_computation | loop fusion | flops 524288 | bytes 3145728 | tf_op jit(solution)/shard_map/div | solution.py:263
  101.9 1.8 %copy.9 = f32[32,2,4096]{2,1,0:T(2,128)} copy(f32[32,2,4096]{2,0,1:T(8,128)S(1)} %maximum_divide_fusion) | data formatting | bytes 2097152 | tf_op jit(solution)/shard_map/div | solution.py:263
Async XLA Ops:
  0.0 100.0 %copy-start = (f32[32,2,4096]{2,1,0:T(2,128)S(1)}, f32[32,2,4096]{2,1,0:T(2,128)}, u32[]{:S(2)}) copy-start(f32[32,2,4096]{2,1,0:T(2,128)} %param.9) | copy-start | bytes 3145732
